TPU v7x, 32 devices: a whole 2x2x4 slice. The times are simulated.
32 devices in a mesh: aa: 4 (over z), ba: 8 (over y, x, core).
Axes of the slice: x: 2, y: 2, z: 4, core: 2. Of those that a mesh axis runs over, the one named last changes fastest.
Arguments:
- feats: bfloat16 [4, 32, 128, 256], P('aa', 'ba'), may hold values from -6 to 6
- conv_one: bfloat16 [3, 3, 3, 256, 256], replicated, may hold values from -0.078125 to 0.078125
- bias_one: float32 [256], replicated, may hold values from -3 to 3
- conv_two: bfloat16 [3, 3, 3, 256, 256], replicated, may hold values from -0.078125 to 0.078125
- bias_two: float32 [256], replicated, may hold values from -3 to 3
- patch_weight: bfloat16 [2, 2, 256, 128], replicated, may hold values from -0.1875 to 0.1875
- patch_bias: float32 [128], replicated, may hold values from -3 to 3
- embed_weight: bfloat16 [128, 2048], replicated, may hold values from -0.5 to 0.5
- embed_bias: float32 [2048], replicated, may hold values from -6 to 6
- norm_gain: float32 [2048], replicated, may hold values from 0.1 to 1.9
- w_query: bfloat16 [2048, 2048], P(None, 'ba'), may hold values from -2 to 2
- w_key: bfloat16 [2048, 2048], P(None, 'ba'), may hold values from -2 to 2
- w_value: bfloat16 [2048, 2048], P(None, 'ba'), may hold values from -0.125 to 0.125
- w_velocity: bfloat16 [2048, 128], P('ba'), may hold values from -0.5 to 0.5
Outputs:
- velocity: float32 [4096, 128], P(('aa', 'ba'))
All inputs are finite; a program needn't handle non-finite values.
Results may differ from a plain program's by a relative error of at most 0.035.
Values may be sent and summed in bfloat16 or wider, within the bound.
A program may use at most 128 MiB of HBM per device.

v0:
```python
import math
import jax
import jax.numpy as jnp
from jax import lax
from jax.sharding import PartitionSpec as P

HEAD_DIM = 64


def with_halo(cells, sides, width):
    for axis, dim in sides:
        count = lax.axis_size(axis)
        ends = count - 1
        head = lax.slice_in_dim(cells, 0, width, axis=dim)
        tail = lax.slice_in_dim(cells, cells.shape[dim] - width, cells.shape[dim], axis=dim)
        cells = jnp.concatenate(
            [
                lax.ppermute(tail, axis, [(i, (i + 1) % count) for i in range(ends)]),
                cells,
                lax.ppermute(head, axis, [((i + 1) % count, i) for i in range(ends)]),
            ],
            axis=dim,
        )
    return cells


def convolve(field, kernel, bias):
    frames, rows, width, chans = field.shape
    padded = with_halo(field, (("aa", 0), ("ba", 1)), 1)
    padded = jnp.pad(padded, ((0, 0), (0, 0), (1, 1), (0, 0)))
    total = jnp.zeros((frames * rows * width, kernel.shape[-1]), jnp.float32)
    for shift_t in range(3):
        for shift_r in range(3):
            window = padded[shift_t : shift_t + frames, shift_r : shift_r + rows]
            stacked = jnp.concatenate(
                [window[:, :, shift_w : shift_w + width] for shift_w in range(3)], axis=-1
            )
            total = total + jnp.dot(
                stacked.reshape(-1, 3 * chans),
                kernel[shift_t, shift_r].reshape(3 * chans, -1),
                preferred_element_type=jnp.float32,
            )
    return (total + bias).reshape(frames, rows, width, -1)


def patchify(field, weight, bias):
    frames, rows, width, chans = field.shape
    blocks = (
        field.reshape(frames, rows // 2, 2, width // 2, 2, chans)
        .transpose(0, 1, 3, 2, 4, 5)
        .reshape(-1, 4 * chans)
    )
    return (
        jnp.dot(blocks, weight.reshape(4 * chans, -1), preferred_element_type=jnp.float32) + bias
    ).astype(jnp.bfloat16)


def normalize(latent_rows, embed_weight, embed_bias, norm_gain):
    hidden = jnp.dot(latent_rows, embed_weight, preferred_element_type=jnp.float32) + embed_bias
    center = hidden - hidden.mean(-1, keepdims=True)
    spread = (center * center).mean(-1, keepdims=True)
    return (center * lax.rsqrt(spread + 1e-05) * norm_gain).astype(jnp.bfloat16)


def attend(queries, keys, values):
    rows, width = queries.shape
    heads = width // HEAD_DIM
    scale = HEAD_DIM ** (-0.5)
    query_heads = queries.reshape(rows, heads, HEAD_DIM)
    start_state = (
        jnp.full((heads, rows), -jnp.inf, jnp.float32),
        jnp.zeros((heads, rows), jnp.float32),
        jnp.zeros((rows, heads, HEAD_DIM), jnp.float32),
    )
    key_rows = lax.all_gather(keys, "aa", axis=0, tiled=True)
    value_rows = lax.all_gather(values, "aa", axis=0, tiled=True)
    count = key_rows.shape[0]
    block = math.gcd(count, 1024)

    def one_step(index, state):
        best, denom, accum = state
        key_block = lax.dynamic_slice_in_dim(key_rows, index * block, block, 0).reshape(
            block, heads, HEAD_DIM
        )
        value_block = lax.dynamic_slice_in_dim(value_rows, index * block, block, 0).reshape(
            block, heads, HEAD_DIM
        )
        scores = (
            jnp.einsum("qhd,khd->hqk", query_heads, key_block, preferred_element_type=jnp.float32)
            * scale
        )
        peak = jnp.maximum(best, scores.max(-1))
        probs = jnp.exp(scores - peak[..., None])
        fade = jnp.exp(best - peak)
        denom = denom * fade + probs.sum(-1)
        accum = accum * fade.T[..., None] + jnp.einsum(
            "hqk,khd->qhd",
            probs.astype(jnp.bfloat16),
            value_block,
            preferred_element_type=jnp.float32,
        )
        return (peak, denom, accum)

    best, denom, accum = lax.fori_loop(0, count // block, one_step, start_state)
    return (accum / denom.T[..., None]).reshape(rows, width).astype(jnp.bfloat16)


def on_device(
    feats,
    conv_one,
    bias_one,
    conv_two,
    bias_two,
    patch_weight,
    patch_bias,
    embed_weight,
    embed_bias,
    norm_gain,
    w_query,
    w_key,
    w_value,
    w_velocity,
):
    first = jax.nn.gelu(convolve(feats, conv_one, bias_one), approximate=False).astype(jnp.bfloat16)
    second = (
        first.astype(jnp.float32)
        + jax.nn.gelu(convolve(first, conv_two, bias_two), approximate=False)
    ).astype(jnp.bfloat16)
    latents = patchify(second, patch_weight, patch_bias)
    width = w_query.shape[1]
    w_joined = jnp.concatenate([w_query, w_key, w_value], axis=1)
    joined = jnp.dot(
        normalize(
            lax.all_gather(latents, "ba", axis=0, tiled=True), embed_weight, embed_bias, norm_gain
        ),
        w_joined,
        preferred_element_type=jnp.float32,
    ).astype(jnp.bfloat16)
    attended = attend(joined[:, :width], joined[:, width : 2 * width], joined[:, 2 * width :])
    return lax.psum_scatter(
        jnp.dot(attended, w_velocity, preferred_element_type=jnp.float32).astype(jnp.bfloat16),
        "ba",
        scatter_dimension=0,
        tiled=True,
    ).astype(jnp.float32)


def solution(mesh):
    return jax.shard_map(
        on_device,
        mesh=mesh,
        in_specs=(
            P("aa", "ba", None, None),
            P(),
            P(),
            P(),
            P(),
            P(),
            P(),
            P(),
            P(),
            P(),
            P(None, "ba"),
            P(None, "ba"),
            P(None, "ba"),
            P("ba", None),
        ),
        out_specs=P(("aa", "ba"), None),
        check_vma=False,
    )
```

profile of v0, /device:TPU:0, one launch (start us, length us, event | category | flops | bytes accessed | tf_op | source)
XLA Modules:
  0.0 332.6 jit_solution(549942878547130094)
XLA Ops:
  6.5 5.1 %collective-permute-start = (bf16[1,4,128,256]{3,2,1,0:T(8,128)(2,1)}, bf16[1,4,128,256]{3,2,1,0:T(8,128)(2,1)S(1)}, u32[]{:S(2)}, u32[]{:S(2)}) collective-permute-start(bf16[1,4,128,256]{3,2,1,0:T(8,128)(2,1)} %param.16), channel_id=1, source_target_pairs={{0,8},{8,16},{16,24},{1,9},{9,17},{17,25},{2,10},{10,18},{18,26},{... | collective-permute-start | bytes 786440 | tf_op jit(solution)/shard_map/ppermute | solution.py:18
  12.9 4.5 %collective-permute-done = bf16[1,4,128,256]{3,2,1,0:T(8,128)(2,1)S(1)} collective-permute-done((bf16[1,4,128,256]{3,2,1,0:T(8,128)(2,1)}, bf16[1,4,128,256]{3,2,1,0:T(8,128)(2,1)S(1)}, u32[]{:S(2)}, u32[]{:S(2)}) %collective-permute-start) | collective-permute-done | bytes 262176 | tf_op jit(solution)/shard_map/ppermute | solution.py:18
  18.5 3.0 collective-permute-done.1
  24.2 2.2 fusion.102
  26.4 1.6 collective-permute-done.3
  33.6 2.1 fusion.69
  36.8 3.5 %collective-permute-start.4 = (bf16[1,4,128,256]{3,2,1,0:T(8,128)(2,1)S(1)}, bf16[1,4,128,256]{3,2,1,0:T(8,128)(2,1)S(1)}, u32[]{:S(2)}, u32[]{:S(2)}) collective-permute-start(bf16[1,4,128,256]{3,2,1,0:T(8,128)(2,1)S(1)} %fusion.66), channel_id=1, source_target_pairs={{0,8},{8,16},{16,24},{1,9},{9,17},{17,25},{2,10},{10,18},{18,26},{... | collective-permute-start | bytes 786440 | tf_op jit(solution)/shard_map/ppermute | solution.py:18
  41.6 2.6 collective-permute-done.4
  44.1 4.4 %collective-permute-done.5 = bf16[1,4,128,256]{3,2,1,0:T(8,128)(2,1)S(1)} collective-permute-done((bf16[1,4,128,256]{3,2,1,0:T(8,128)(2,1)S(1)}, bf16[1,4,128,256]{3,2,1,0:T(8,128)(2,1)S(1)}, u32[]{:S(2)}, u32[]{:S(2)}) %collective-permute-start.5) | collective-permute-done | bytes 262176 | tf_op jit(solution)/shard_map/ppermute | solution.py:20
  49.3 5.3 %collective-permute-start.6 = (bf16[3,1,128,256]{3,2,1,0:T(8,128)(2,1)}, bf16[3,1,128,256]{3,2,1,0:T(8,128)(2,1)}, u32[]{:S(2)}, u32[]{:S(2)}) collective-permute-start(bf16[3,1,128,256]{3,2,1,0:T(8,128)(2,1)} %get-tuple-element.246), channel_id=1, source_target_pairs={{0,1},{1,2},{2,3},{3,4},{4,5},{5,6},{6,7},{8,9},{9,10},{10,11},{11... | collective-permute-start | bytes 589832 | tf_op jit(solution)/shard_map/ppermute | solution.py:18
  54.6 1.5 collective-permute-start.7
  56.1 1.7 fusion.101
  59.6 1.5 select_maximum_fusion.1
  70.8 2.2 fusion.98
  74.7 15.0 %all_gather.9 = bf16[1024,128]{1,0:T(8,128)(2,1)S(1)} all-gather(bf16[128,128]{1,0:T(8,128)(2,1)S(1)} %fusion.31), channel_id=1, replica_groups=mesh['aa'=4,'ba'=8] {'ba'}, dimensions={0}, use_global_device_ids=true | all-gather | bytes 294912 | tf_op jit(solution)/shard_map/all_gather | solution.py:134
  92.9 4.3 %fusion.25 = bf16[1024,768]{0,1:T(8,128)(2,1)S(1)} fusion(bf16[2048,256]{1,0:T(8,128)(2,1)S(1)} %copy-done.16, bf16[2048,256]{1,0:T(8,128)(2,1)S(1)} %copy-done.17, bf16[2048,256]{1,0:T(8,128)(2,1)S(1)} %copy-done.18, f32[1024,2048]{1,0:T(8,128)S(1)} %get-tuple-element.255, f32[2048]{0:T(1024)S(1)} %copy-done.19, f32[1024]{0:T(1024)S(1)} %add_rsqrt_fusion, ...), kind=kOutput, calls=%fused_computation.33 | convolution fusion | flops 3241934848 | bytes 13131776 | tf_op jit(solution)/shard_map/dot_general | solution.py:132
  99.4 43.0 %all-gather.3.cloned.1.call-done = bf16[4096,256]{0,1:T(8,128)(2,1)} async-done(((bf16[1024,256]{0,1:T(8,128)(2,1)}), bf16[4096,256]{0,1:T(8,128)(2,1)}) %all-gather.3.cloned.1.call-update) | async-done | bytes 2097168 | tf_op jit(solution)/shard_map/all_gather | solution.py:75
  142.4 46.1 %all-gather.5.cloned.1.call-done = bf16[4096,256]{0,1:T(8,128)(2,1)} async-done(((bf16[1024,256]{0,1:T(8,128)(2,1)}), bf16[4096,256]{0,1:T(8,128)(2,1)}) %all-gather.5.cloned.1.call-update) | async-done | bytes 2097168 | tf_op jit(solution)/shard_map/all_gather | solution.py:76
  188.4 101.7 %while.18 = (s32[]{:T(128)}, f32[4,1024]{1,0:T(4,128)S(1)}, f32[4,1024]{1,0:T(4,128)S(1)}, f32[1024,4,64]{0,2,1:T(8,128)S(1)}, bf16[4096,256]{0,1:T(8,128)(2,1)}...) while((s32[]{:T(128)}, f32[4,1024]{1,0:T(4,128)S(1)}, ...), condition=%wide.region_5.6_spmd.clone, body=%wide.region_2.5_spmd.clone.sunk | while | flops 1108107264 | bytes 56361128 | solution.py:104
  189.7 8.1 %bitcast_reduce_fusion.2 = (f32[4,1024]{1,0:T(4,128)S(1)}, f32[4,1024,1024]{2,1,0:T(8,128)}) fusion(bf16[1024,4,64]{0,2,1:T(8,128)(2,1)S(1)} %bitcast.131, bf16[1024,4,64]{0,2,1:T(8,128)(2,1)S(1)} %get-tuple-element.340), kind=kOutput, calls=%fused_computation.1.clone.1 | convolution fusion | flops 545255424 | bytes 17842176 | tf_op jit(solution)/shard_map/while/body/eval_jaxpr/qhd,khd->hqk/dot_general | solution.py:89
  197.9 7.4 %fusion.168 = f32[1024,4,64]{0,2,1:T(8,128)S(1)} fusion(bf16[1024,4,64]{0,2,1:T(8,128)(2,1)S(1)} %bitcast.132, f32[4,1024,1024]{2,1,0:T(8,128)} %get-tuple-element.310, f32[4,1024]{1,0:T(4,128)S(1)} %get-tuple-element.336, f32[1024,4,64]{0,2,1:T(8,128)S(1)} %get-tuple-element.327, f32[1024,4]{0,1:T(4,128)S(1)} %get-tuple-element.312, pred[]{:T(512)S(6)} %compare.43), kind=kOutput, calls=%fused_computation.7.clone.1 | convolution fusion | flops 550240256 | bytes 19431424 | tf_op jit(solution)/shard_map/while/body/eval_jaxpr/hqk,khd->qhd/dot_general | solution.py:96
  205.2 8.5 %fusion.166 = f32[4,1024]{1,0:T(4,128)S(1)} fusion(f32[4,1024,1024]{2,1,0:T(8,128)} %get-tuple-element.310, f32[4,1024]{1,0:T(4,128)S(1)} %get-tuple-element.336), kind=kLoop, calls=%fused_computation.4.clone.1 | loop fusion | flops 12578816 | bytes 16809984 | tf_op jit(solution)/shard_map/while/body/eval_jaxpr/reduce_sum | solution.py:95
  215.1 8.1 %bitcast_reduce_fusion.2 = (f32[4,1024]{1,0:T(4,128)S(1)}, f32[4,1024,1024]{2,1,0:T(8,128)}) fusion(bf16[1024,4,64]{0,2,1:T(8,128)(2,1)S(1)} %bitcast.131, bf16[1024,4,64]{0,2,1:T(8,128)(2,1)S(1)} %get-tuple-element.340), kind=kOutput, calls=%fused_computation.1.clone.1 | convolution fusion | flops 545255424 | bytes 17842176 | tf_op jit(solution)/shard_map/while/body/eval_jaxpr/qhd,khd->hqk/dot_general | solution.py:89
  223.3 7.4 %fusion.168 = f32[1024,4,64]{0,2,1:T(8,128)S(1)} fusion(bf16[1024,4,64]{0,2,1:T(8,128)(2,1)S(1)} %bitcast.132, f32[4,1024,1024]{2,1,0:T(8,128)} %get-tuple-element.310, f32[4,1024]{1,0:T(4,128)S(1)} %get-tuple-element.336, f32[1024,4,64]{0,2,1:T(8,128)S(1)} %get-tuple-element.327, f32[1024,4]{0,1:T(4,128)S(1)} %get-tuple-element.312, pred[]{:T(512)S(6)} %compare.43), kind=kOutput, calls=%fused_computation.7.clone.1 | convolution fusion | flops 550240256 | bytes 19431424 | tf_op jit(solution)/shard_map/while/body/eval_jaxpr/hqk,khd->qhd/dot_general | solution.py:96
  230.7 8.5 %fusion.166 = f32[4,1024]{1,0:T(4,128)S(1)} fusion(f32[4,1024,1024]{2,1,0:T(8,128)} %get-tuple-element.310, f32[4,1024]{1,0:T(4,128)S(1)} %get-tuple-element.336), kind=kLoop, calls=%fused_computation.4.clone.1 | loop fusion | flops 12578816 | bytes 16809984 | tf_op jit(solution)/shard_map/while/body/eval_jaxpr/reduce_sum | solution.py:95
  240.5 8.1 %bitcast_reduce_fusion.2 = (f32[4,1024]{1,0:T(4,128)S(1)}, f32[4,1024,1024]{2,1,0:T(8,128)}) fusion(bf16[1024,4,64]{0,2,1:T(8,128)(2,1)S(1)} %bitcast.131, bf16[1024,4,64]{0,2,1:T(8,128)(2,1)S(1)} %get-tuple-element.340), kind=kOutput, calls=%fused_computation.1.clone.1 | convolution fusion | flops 545255424 | bytes 17842176 | tf_op jit(solution)/shard_map/while/body/eval_jaxpr/qhd,khd->hqk/dot_general | solution.py:89
  248.7 7.4 %fusion.168 = f32[1024,4,64]{0,2,1:T(8,128)S(1)} fusion(bf16[1024,4,64]{0,2,1:T(8,128)(2,1)S(1)} %bitcast.132, f32[4,1024,1024]{2,1,0:T(8,128)} %get-tuple-element.310, f32[4,1024]{1,0:T(4,128)S(1)} %get-tuple-element.336, f32[1024,4,64]{0,2,1:T(8,128)S(1)} %get-tuple-element.327, f32[1024,4]{0,1:T(4,128)S(1)} %get-tuple-element.312, pred[]{:T(512)S(6)} %compare.43), kind=kOutput, calls=%fused_computation.7.clone.1 | convolution fusion | flops 550240256 | bytes 19431424 | tf_op jit(solution)/shard_map/while/body/eval_jaxpr/hqk,khd->qhd/dot_general | solution.py:96
  256.1 8.5 %fusion.166 = f32[4,1024]{1,0:T(4,128)S(1)} fusion(f32[4,1024,1024]{2,1,0:T(8,128)} %get-tuple-element.310, f32[4,1024]{1,0:T(4,128)S(1)} %get-tuple-element.336), kind=kLoop, calls=%fused_computation.4.clone.1 | loop fusion | flops 12578816 | bytes 16809984 | tf_op jit(solution)/shard_map/while/body/eval_jaxpr/reduce_sum | solution.py:95
  266.0 8.1 %bitcast_reduce_fusion.2 = (f32[4,1024]{1,0:T(4,128)S(1)}, f32[4,1024,1024]{2,1,0:T(8,128)}) fusion(bf16[1024,4,64]{0,2,1:T(8,128)(2,1)S(1)} %bitcast.131, bf16[1024,4,64]{0,2,1:T(8,128)(2,1)S(1)} %get-tuple-element.340), kind=kOutput, calls=%fused_computation.1.clone.1 | convolution fusion | flops 545255424 | bytes 17842176 | tf_op jit(solution)/shard_map/while/body/eval_jaxpr/qhd,khd->hqk/dot_general | solution.py:89
  274.1 7.4 %fusion.168 = f32[1024,4,64]{0,2,1:T(8,128)S(1)} fusion(bf16[1024,4,64]{0,2,1:T(8,128)(2,1)S(1)} %bitcast.132, f32[4,1024,1024]{2,1,0:T(8,128)} %get-tuple-element.310, f32[4,1024]{1,0:T(4,128)S(1)} %get-tuple-element.336, f32[1024,4,64]{0,2,1:T(8,128)S(1)} %get-tuple-element.327, f32[1024,4]{0,1:T(4,128)S(1)} %get-tuple-element.312, pred[]{:T(512)S(6)} %compare.43), kind=kOutput, calls=%fused_computation.7.clone.1 | convolution fusion | flops 550240256 | bytes 19431424 | tf_op jit(solution)/shard_map/while/body/eval_jaxpr/hqk,khd->qhd/dot_general | solution.py:96
  281.5 8.5 %fusion.166 = f32[4,1024]{1,0:T(4,128)S(1)} fusion(f32[4,1024,1024]{2,1,0:T(8,128)} %get-tuple-element.310, f32[4,1024]{1,0:T(4,128)S(1)} %get-tuple-element.336), kind=kLoop, calls=%fused_computation.4.clone.1 | loop fusion | flops 12578816 | bytes 16809984 | tf_op jit(solution)/shard_map/while/body/eval_jaxpr/reduce_sum | solution.py:95
  292.0 32.6 %reduce-scatter.2.cloned.1.call-done = bf16[128,128]{1,0:T(8,128)(2,1)} async-done(((bf16[1024,128]{1,0:T(8,128)(2,1)}), bf16[128,128]{1,0:T(8,128)(2,1)}) %reduce-scatter.2.cloned.1.call-update) | async-done | bytes 32784 | tf_op jit(solution)/shard_map/reduce_scatter | solution.py:140
  (124 shorter events, 40.4 us)
Async XLA Ops:
  6.5 83.1 %copy-start = (bf16[128,2048]{1,0:T(8,128)(2,1)S(1)}, bf16[128,2048]{1,0:T(8,128)(2,1)}, u32[]{:S(2)}) copy-start(bf16[128,2048]{1,0:T(8,128)(2,1)} %param.23) | copy-start | bytes 1572868
  6.5 135.8 %all-gather.3.cloned.1.call-start = ((), (), s32[]{:S(2)}) async-start(), calls=%async_computation.1 | async-start | bytes 2621440 | tf_op jit(solution)/shard_map/all_gather | solution.py:75
  6.5 10.9 %collective-permute-start = (bf16[1,4,128,256]{3,2,1,0:T(8,128)(2,1)}, bf16[1,4,128,256]{3,2,1,0:T(8,128)(2,1)S(1)}, u32[]{:S(2)}, u32[]{:S(2)}) collective-permute-start(bf16[1,4,128,256]{3,2,1,0:T(8,128)(2,1)} %param.16), channel_id=1, source_target_pairs={{0,8},{8,16},{16,24},{1,9},{9,17},{17,25},{2,10},{10,18},{18,26},{... | collective-permute-start | bytes 786440 | tf_op jit(solution)/shard_map/ppermute | solution.py:18
  11.6 9.9 %collective-permute-start.1 = (bf16[1,4,128,256]{3,2,1,0:T(8,128)(2,1)}, bf16[1,4,128,256]{3,2,1,0:T(8,128)(2,1)S(1)}, u32[]{:S(2)}, u32[]{:S(2)}) collective-permute-start(bf16[1,4,128,256]{3,2,1,0:T(8,128)(2,1)} %param.16), channel_id=1, source_target_pairs={{8,0},{16,8},{24,16},{9,1},{17,9},{25,17},{10,2},{18,10},{26,18},{... | collective-permute-start | bytes 786440 | tf_op jit(solution)/shard_map/ppermute | solution.py:20
  21.6 4.8 %collective-permute-start.2 = (bf16[3,1,128,256]{3,2,1,0:T(8,128)(2,1)S(1)}, bf16[3,1,128,256]{3,2,1,0:T(8,128)(2,1)S(1)}, u32[]{:S(2)}, u32[]{:S(2)}) collective-permute-start(bf16[3,1,128,256]{3,2,1,0:T(8,128)(2,1)S(1)} %get-tuple-element.248), channel_id=1, source_target_pairs={{0,1},{1,2},{2,3},{3,4},{4,5},{5,6},{6,7},{8,9},{9,10},{10,11},{11... | collective-permute-start | bytes 589832 | tf_op jit(solution)/shard_map/ppermute | solution.py:18
  22.9 5.1 %collective-permute-start.3 = (bf16[3,1,128,256]{3,2,1,0:T(8,128)(2,1)S(1)}, bf16[3,1,128,256]{3,2,1,0:T(8,128)(2,1)S(1)}, u32[]{:S(2)}, u32[]{:S(2)}) collective-permute-start(bf16[3,1,128,256]{3,2,1,0:T(8,128)(2,1)S(1)} %get-tuple-element.247), channel_id=1, source_target_pairs={{1,0},{2,1},{3,2},{4,3},{5,4},{6,5},{7,6},{9,8},{10,9},{11,10},{12... | collective-permute-start | bytes 589832 | tf_op jit(solution)/shard_map/ppermute | solution.py:20
  28.5 1.0 copy-start.10
  33.6 22.5 %copy-start.2 = (bf16[3,3,3,256,256]{4,3,2,1,0:T(8,128)(2,1)S(1)}, bf16[3,3,3,256,256]{4,3,2,1,0:T(8,128)(2,1)}, u32[]{:S(2)}) copy-start(bf16[3,3,3,256,256]{4,3,2,1,0:T(8,128)(2,1)} %param.19) | copy-start | bytes 10616836
  36.8 7.3 %collective-permute-start.4 = (bf16[1,4,128,256]{3,2,1,0:T(8,128)(2,1)S(1)}, bf16[1,4,128,256]{3,2,1,0:T(8,128)(2,1)S(1)}, u32[]{:S(2)}, u32[]{:S(2)}) collective-permute-start(bf16[1,4,128,256]{3,2,1,0:T(8,128)(2,1)S(1)} %fusion.66), channel_id=1, source_target_pairs={{0,8},{8,16},{16,24},{1,9},{9,17},{17,25},{2,10},{10,18},{18,26},{... | collective-permute-start | bytes 786440 | tf_op jit(solution)/shard_map/ppermute | solution.py:18
  40.3 8.3 %collective-permute-start.5 = (bf16[1,4,128,256]{3,2,1,0:T(8,128)(2,1)S(1)}, bf16[1,4,128,256]{3,2,1,0:T(8,128)(2,1)S(1)}, u32[]{:S(2)}, u32[]{:S(2)}) collective-permute-start(bf16[1,4,128,256]{3,2,1,0:T(8,128)(2,1)S(1)} %fusion.66), channel_id=1, source_target_pairs={{8,0},{16,8},{24,16},{9,1},{17,9},{25,17},{10,2},{18,10},{26,18},{... | collective-permute-start | bytes 786440 | tf_op jit(solution)/shard_map/ppermute | solution.py:20
  49.3 9.1 %collective-permute-start.6 = (bf16[3,1,128,256]{3,2,1,0:T(8,128)(2,1)}, bf16[3,1,128,256]{3,2,1,0:T(8,128)(2,1)}, u32[]{:S(2)}, u32[]{:S(2)}) collective-permute-start(bf16[3,1,128,256]{3,2,1,0:T(8,128)(2,1)} %get-tuple-element.246), channel_id=1, source_target_pairs={{0,1},{1,2},{2,3},{3,4},{4,5},{5,6},{6,7},{8,9},{9,10},{10,11},{11... | collective-permute-start | bytes 589832 | tf_op jit(solution)/shard_map/ppermute | solution.py:18
  54.6 5.0 %collective-permute-start.7 = (bf16[3,1,128,256]{3,2,1,0:T(8,128)(2,1)}, bf16[3,1,128,256]{3,2,1,0:T(8,128)(2,1)S(1)}, u32[]{:S(2)}, u32[]{:S(2)}) collective-permute-start(bf16[3,1,128,256]{3,2,1,0:T(8,128)(2,1)} %get-tuple-element.245), channel_id=1, source_target_pairs={{1,0},{2,1},{3,2},{4,3},{5,4},{6,5},{7,6},{9,8},{10,9},{11,10},{12... | collective-permute-start | bytes 589832 | tf_op jit(solution)/shard_map/ppermute | solution.py:20
  62.0 1.1 copy-start.9
  63.1 1.0 copy-start.8
  64.5 1.0 copy-start.7
  64.8 1.1 copy-start.6
  65.9 1.0 copy-start.11
  65.9 1.1 copy-start.21
  66.3 1.1 copy-start.5
  67.3 1.0 copy-start.4
  68.3 1.0 copy-start.3
  68.7 1.0 copy-start.14
  70.8 2.7 copy-start.15
  70.8 18.9 %copy-start.12 = (f32[2048]{0:T(1024)S(1)}, f32[2048]{0:T(1024)}, u32[]{:S(2)}) copy-start(f32[2048]{0:T(1024)} %param.24) | copy-start | bytes 24580
  91.0 1.3 copy-start.16
  91.0 1.5 copy-start.17
  91.0 1.8 copy-start.18
  91.0 1.8 copy-start.19
  98.3 90.1 %all-gather.5.cloned.1.call-start = ((), (), s32[]{:S(2)}) async-start(), calls=%async_computation.2 | async-start | bytes 2621440 | tf_op jit(solution)/shard_map/all_gather | solution.py:76
  99.1 225.6 %reduce-scatter.2.cloned.1.call-start = ((), (), s32[]{:S(2)}) async-start(), calls=%async_computation.3 | async-start | bytes 294912 | tf_op jit(solution)/shard_map/reduce_scatter | solution.py:140
  290.1 0.8 copy-start.13
  290.1 35.9 %copy-start.1 = (bf16[128,2048]{1,0:T(8,128)(2,1)S(1)}, bf16[128,2048]{1,0:T(8,128)(2,1)}, u32[]{:S(2)}) copy-start(bf16[128,2048]{1,0:T(8,128)(2,1)} %param.23) | copy-start | bytes 1572868
  (1 other events, 0.7 us)
Sparse Core Ops, SparseCore 0:
  98.4 43.8 all-gather.2
  143.9 44.4 all-gather.4
  292.1 32.4 reduce-scatter.1
where the time goes:
time: 334 us; the launch traced here: 333 us
  waiting for transfers between devices  140 us (42%)
  matrix products  78.4 us (23%)
  other arithmetic  45.5 us (14%)
  starting transfers between devices  20.9 us (6%)
  local copies, waits for them, and re-layouts  19.1 us (6%)
  blocking collectives  15 us (4%)
  between operations  13.7 us (4%)
    all_gather x1, waiting for transfers between devices, attend(): value_rows = lax.all_gather(values, 'aa', axis=0, tiled=True)  46.1 us
    all_gather x1, waiting for transfers between devices, attend(): key_rows = lax.all_gather(keys, 'aa', axis=0, tiled=True)  43 us
    reduce_sum x4, other arithmetic, one_step(): denom = denom * fade + probs.sum(-1)  34.1 us
    reduce_scatter x1, waiting for transfers between devices, on_device(): lax.psum_scatter(jnp.dot(attended, w_velocity, preferred_element_type=jnp...  32.6 us
    dot_general x4, matrix products, one_step(): jnp.einsum('qhd,khd->hqk', query_heads, key_block, preferred_element_type...  32.6 us
    dot_general x4, matrix products, one_step(): jnp.einsum('hqk,khd->qhd', probs.astype(jnp.bfloat16), value_block, prefe...  29.5 us
    ppermute x4, starting transfers between devices, with_halo(): lax.ppermute(tail, axis, [(i, (i + 1) % count) for i in range(ends)])  15.2 us
    all_gather x1, blocking collectives, on_device(): lax.all_gather(latents, 'ba', axis=0, tiled=True)  15 us
  transfers between devices with their start and end apart: 11, of which 9 were waited for; matrix products, arithmetic and copies ran while one was open for 2% of the time, Pallas kernels for 0%

commit v1 on v0

--- a/solution.py
+++ b/solution.py
@@ -5,6 +5,19 @@
 from jax.sharding import PartitionSpec as P
 
 HEAD_DIM = 64
+
+
+def gather_around(x, axis, dim):
+    ways = lax.axis_size(axis)
+    up = [(d, (d + 1) % ways) for d in range(ways)]
+    down = [(d, (d - 1) % ways) for d in range(ways)]
+    earlier, later = ([x], [x])
+    for _ in range(ways // 2):
+        earlier.append(lax.ppermute(earlier[-1], axis, up))
+    for _ in range((ways - 1) // 2):
+        later.append(lax.ppermute(later[-1], axis, down))
+    line = jnp.concatenate([*earlier[::-1], *later[1:]], axis=dim)
+    return jnp.roll(line, (lax.axis_index(axis) - ways // 2) * x.shape[dim], axis=dim)
 
 
 def with_halo(cells, sides, width):
@@ -73,7 +86,7 @@
         jnp.zeros((rows, heads, HEAD_DIM), jnp.float32),
     )
     key_rows = lax.all_gather(keys, "aa", axis=0, tiled=True)
-    value_rows = lax.all_gather(values, "aa", axis=0, tiled=True)
+    value_rows = gather_around(values, "aa", 0)
     count = key_rows.shape[0]
     block = math.gcd(count, 1024)
 

time: 334 us -> 330 us (0.988)
  waiting for transfers between devices: 140 us -> 126 us
  local copies, waits for them, and re-layouts: 19.1 us -> 25.2 us
  starting transfers between devices: 20.9 us -> 26.3 us
    all_gather x1 -> x0, waiting for transfers between devices: 46.1 us -> none  [attend(): value_rows = lax.all_gather(values, 'aa', axis=0, tiled=True)]
    ppermute x0 -> x3, waiting for transfers between devices: none -> 35 us  [the longest x2 27.2 us: gather_around(): earlier.append(lax.ppermute(earlier[-1], axis, up))]
    ppermute x0 -> x3, starting transfers between devices: none -> 5.45 us  [the longest x1 3.82 us: gather_around(): later.append(lax.ppermute(later[-1], axis, down))]
    unnamed x46 -> x61, local copies, waits for them, and re-layouts: 5.63 us -> 8.73 us
  transfers between devices with their start and end apart: 11 -> 13, of which waited for: 9 -> 11; matrix products, arithmetic and copies ran while one was open for 2% -> 3% of each run, Pallas kernels for 0% -> 0%
where the time goes in v1:
time: 330 us; the launch traced here: 329 us
  waiting for transfers between devices  126 us (38%)
  matrix products  77.5 us (23%)
  other arithmetic  45.5 us (14%)
  starting transfers between devices  26.3 us (8%)
  local copies, waits for them, and re-layouts  25.2 us (8%)
  blocking collectives  15 us (5%)
  between operations  14.2 us (4%)
    all_gather x1, waiting for transfers between devices, attend(): key_rows = lax.all_gather(keys, 'aa', axis=0, tiled=True)  40.5 us
    reduce_sum x4, other arithmetic, one_step(): denom = denom * fade + probs.sum(-1)  34.1 us
    reduce_scatter x1, waiting for transfers between devices, on_device(): lax.psum_scatter(jnp.dot(attended, w_velocity, preferred_element_type=jnp...  32.6 us
    dot_general x4, matrix products, one_step(): jnp.einsum('qhd,khd->hqk', query_heads, key_block, preferred_element_type...  32.6 us
    dot_general x4, matrix products, one_step(): jnp.einsum('hqk,khd->qhd', probs.astype(jnp.bfloat16), value_block, prefe...  29.5 us
    ppermute x2, waiting for transfers between devices, gather_around(): earlier.append(lax.ppermute(earlier[-1], axis, up))  27.2 us
    ppermute x4, starting transfers between devices, with_halo(): lax.ppermute(tail, axis, [(i, (i + 1) % count) for i in range(ends)])  15.2 us
    all_gather x1, blocking collectives, on_device(): lax.all_gather(latents, 'ba', axis=0, tiled=True)  15 us
  transfers between devices with their start and end apart: 13, of which 11 were waited for; matrix products, arithmetic and copies ran while one was open for 3% of the time, Pallas kernels for 0%

profile of v1, /device:TPU:0, one launch (start us, length us, event | category | flops | bytes accessed | tf_op | source)
XLA Modules:
  0.0 329.4 jit_solution(3581667895422941268)
XLA Ops:
  6.5 5.1 %collective-permute-start = (bf16[1,4,128,256]{3,2,1,0:T(8,128)(2,1)}, bf16[1,4,128,256]{3,2,1,0:T(8,128)(2,1)S(1)}, u32[]{:S(2)}, u32[]{:S(2)}) collective-permute-start(bf16[1,4,128,256]{3,2,1,0:T(8,128)(2,1)} %param.16), channel_id=1, source_target_pairs={{0,8},{8,16},{16,24},{1,9},{9,17},{17,25},{2,10},{10,18},{18,26},{... | collective-permute-start | bytes 786440 | tf_op jit(solution)/shard_map/ppermute | solution.py:31
  12.9 4.5 %collective-permute-done = bf16[1,4,128,256]{3,2,1,0:T(8,128)(2,1)S(1)} collective-permute-done((bf16[1,4,128,256]{3,2,1,0:T(8,128)(2,1)}, bf16[1,4,128,256]{3,2,1,0:T(8,128)(2,1)S(1)}, u32[]{:S(2)}, u32[]{:S(2)}) %collective-permute-start) | collective-permute-done | bytes 262176 | tf_op jit(solution)/shard_map/ppermute | solution.py:31
  18.5 3.0 collective-permute-done.1
  24.2 2.2 fusion.102
  33.5 2.1 fusion.69
  36.8 3.5 %collective-permute-start.4 = (bf16[1,4,128,256]{3,2,1,0:T(8,128)(2,1)S(1)}, bf16[1,4,128,256]{3,2,1,0:T(8,128)(2,1)S(1)}, u32[]{:S(2)}, u32[]{:S(2)}) collective-permute-start(bf16[1,4,128,256]{3,2,1,0:T(8,128)(2,1)S(1)} %fusion.66), channel_id=1, source_target_pairs={{0,8},{8,16},{16,24},{1,9},{9,17},{17,25},{2,10},{10,18},{18,26},{... | collective-permute-start | bytes 786440 | tf_op jit(solution)/shard_map/ppermute | solution.py:31
  41.6 2.6 collective-permute-done.4
  44.1 4.4 %collective-permute-done.5 = bf16[1,4,128,256]{3,2,1,0:T(8,128)(2,1)S(1)} collective-permute-done((bf16[1,4,128,256]{3,2,1,0:T(8,128)(2,1)S(1)}, bf16[1,4,128,256]{3,2,1,0:T(8,128)(2,1)S(1)}, u32[]{:S(2)}, u32[]{:S(2)}) %collective-permute-start.5) | collective-permute-done | bytes 262176 | tf_op jit(solution)/shard_map/ppermute | solution.py:33
  49.3 5.3 %collective-permute-start.6 = (bf16[3,1,128,256]{3,2,1,0:T(8,128)(2,1)}, bf16[3,1,128,256]{3,2,1,0:T(8,128)(2,1)}, u32[]{:S(2)}, u32[]{:S(2)}) collective-permute-start(bf16[3,1,128,256]{3,2,1,0:T(8,128)(2,1)} %get-tuple-element.246), channel_id=1, source_target_pairs={{0,1},{1,2},{2,3},{3,4},{4,5},{5,6},{6,7},{8,9},{9,10},{10,11},{11... | collective-permute-start | bytes 589832 | tf_op jit(solution)/shard_map/ppermute | solution.py:31
  70.9 2.2 fusion.98
  73.8 15.0 %all_gather.6 = bf16[1024,128]{1,0:T(8,128)(2,1)S(1)} all-gather(bf16[128,128]{1,0:T(8,128)(2,1)S(1)} %fusion.31), channel_id=1, replica_groups=mesh['aa'=4,'ba'=8] {'ba'}, dimensions={0}, use_global_device_ids=true | all-gather | bytes 294912 | tf_op jit(solution)/shard_map/all_gather | solution.py:147
  92.1 4.3 %fusion.25 = bf16[1024,768]{0,1:T(8,128)(2,1)S(1)} fusion(bf16[2048,256]{1,0:T(8,128)(2,1)S(1)} %copy-done.20, bf16[2048,256]{1,0:T(8,128)(2,1)S(1)} %copy-done.21, bf16[2048,256]{1,0:T(8,128)(2,1)S(1)} %copy-done.22, f32[1024,2048]{1,0:T(8,128)S(1)} %get-tuple-element.255, f32[2048]{0:T(1024)S(1)} %copy-done.23, f32[1024]{0:T(1024)S(1)} %add_rsqrt_fusion, ...), kind=kOutput, calls=%fused_computation.33 | convolution fusion | flops 3241934848 | bytes 13131776 | tf_op jit(solution)/shard_map/dot_general | solution.py:145
  98.0 14.4 %collective-permute-done.8 = bf16[1024,256]{0,1:T(8,128)(2,1)S(1)} collective-permute-done((bf16[1024,256]{0,1:T(8,128)(2,1)S(1)}, bf16[1024,256]{0,1:T(8,128)(2,1)S(1)}, u32[]{:S(2)}, u32[]{:S(2)}) %collective-permute-start.8) | collective-permute-done | bytes 524320 | tf_op jit(solution)/shard_map/ppermute | solution.py:16
  112.4 3.8 %collective-permute-start.10 = (bf16[1024,256]{0,1:T(8,128)(2,1)S(1)}, bf16[1024,256]{0,1:T(8,128)(2,1)S(1)}, u32[]{:S(2)}, u32[]{:S(2)}) collective-permute-start(bf16[1024,256]{0,1:T(8,128)(2,1)S(1)} %slice.446), channel_id=1, source_target_pairs={{0,24},{8,0},{16,8},{24,16},{1,25},{9,1},{17,9},{25,17},{2,26},{10... | collective-permute-start | bytes 1572872 | tf_op jit(solution)/shard_map/ppermute | solution.py:18
  116.3 12.8 %collective-permute-done.9 = bf16[1024,256]{0,1:T(8,128)(2,1)S(1)} collective-permute-done((bf16[1024,256]{0,1:T(8,128)(2,1)S(1)}, bf16[1024,256]{0,1:T(8,128)(2,1)S(1)}, u32[]{:S(2)}, u32[]{:S(2)}) %collective-permute-start.9) | collective-permute-done | bytes 524320 | tf_op jit(solution)/shard_map/ppermute | solution.py:16
  129.2 7.8 %collective-permute-done.10 = bf16[1024,256]{0,1:T(8,128)(2,1)S(1)} collective-permute-done((bf16[1024,256]{0,1:T(8,128)(2,1)S(1)}, bf16[1024,256]{0,1:T(8,128)(2,1)S(1)}, u32[]{:S(2)}, u32[]{:S(2)}) %collective-permute-start.10) | collective-permute-done | bytes 524320 | tf_op jit(solution)/shard_map/ppermute | solution.py:18
  141.3 3.1 constant_dynamic-slice_fusion.2
  144.5 40.5 %all-gather.2.cloned.1.call-done = bf16[4096,256]{0,1:T(8,128)(2,1)} async-done(((bf16[1024,256]{0,1:T(8,128)(2,1)}), bf16[4096,256]{0,1:T(8,128)(2,1)}) %all-gather.2.cloned.1.call-update) | async-done | bytes 2097168 | tf_op jit(solution)/shard_map/all_gather | solution.py:88
  184.9 101.7 %while.18 = (s32[]{:T(128)}, f32[4,1024]{1,0:T(4,128)S(1)}, f32[4,1024]{1,0:T(4,128)S(1)}, f32[1024,4,64]{0,2,1:T(8,128)S(1)}, bf16[4096,256]{0,1:T(8,128)(2,1)}...) while((s32[]{:T(128)}, f32[4,1024]{1,0:T(4,128)S(1)}, ...), condition=%wide.region_5.6_spmd.clone, body=%wide.region_2.5_spmd.clone.sunk | while | flops 1108107264 | bytes 56361128 | solution.py:117
  186.2 8.1 %bitcast_reduce_fusion.2 = (f32[4,1024]{1,0:T(4,128)S(1)}, f32[4,1024,1024]{2,1,0:T(8,128)}) fusion(bf16[1024,4,64]{0,2,1:T(8,128)(2,1)S(1)} %bitcast.131, bf16[1024,4,64]{0,2,1:T(8,128)(2,1)S(1)} %get-tuple-element.340), kind=kOutput, calls=%fused_computation.1.clone.1 | convolution fusion | flops 545255424 | bytes 17842176 | tf_op jit(solution)/shard_map/while/body/eval_jaxpr/qhd,khd->hqk/dot_general | solution.py:102
  194.4 7.4 %fusion.167 = f32[1024,4,64]{0,2,1:T(8,128)S(1)} fusion(bf16[1024,4,64]{0,2,1:T(8,128)(2,1)S(1)} %bitcast.132, f32[4,1024,1024]{2,1,0:T(8,128)} %get-tuple-element.310, f32[4,1024]{1,0:T(4,128)S(1)} %get-tuple-element.336, f32[1024,4,64]{0,2,1:T(8,128)S(1)} %get-tuple-element.327, f32[1024,4]{0,1:T(4,128)S(1)} %get-tuple-element.312, pred[]{:T(512)S(6)} %compare.44), kind=kOutput, calls=%fused_computation.7.clone.1 | convolution fusion | flops 550240256 | bytes 19431424 | tf_op jit(solution)/shard_map/while/body/eval_jaxpr/hqk,khd->qhd/dot_general | solution.py:109
  201.8 8.5 %fusion.165 = f32[4,1024]{1,0:T(4,128)S(1)} fusion(f32[4,1024,1024]{2,1,0:T(8,128)} %get-tuple-element.310, f32[4,1024]{1,0:T(4,128)S(1)} %get-tuple-element.336), kind=kLoop, calls=%fused_computation.4.clone.1 | loop fusion | flops 12578816 | bytes 16809984 | tf_op jit(solution)/shard_map/while/body/eval_jaxpr/reduce_sum | solution.py:108
  211.6 8.1 %bitcast_reduce_fusion.2 = (f32[4,1024]{1,0:T(4,128)S(1)}, f32[4,1024,1024]{2,1,0:T(8,128)}) fusion(bf16[1024,4,64]{0,2,1:T(8,128)(2,1)S(1)} %bitcast.131, bf16[1024,4,64]{0,2,1:T(8,128)(2,1)S(1)} %get-tuple-element.340), kind=kOutput, calls=%fused_computation.1.clone.1 | convolution fusion | flops 545255424 | bytes 17842176 | tf_op jit(solution)/shard_map/while/body/eval_jaxpr/qhd,khd->hqk/dot_general | solution.py:102
  219.8 7.4 %fusion.167 = f32[1024,4,64]{0,2,1:T(8,128)S(1)} fusion(bf16[1024,4,64]{0,2,1:T(8,128)(2,1)S(1)} %bitcast.132, f32[4,1024,1024]{2,1,0:T(8,128)} %get-tuple-element.310, f32[4,1024]{1,0:T(4,128)S(1)} %get-tuple-element.336, f32[1024,4,64]{0,2,1:T(8,128)S(1)} %get-tuple-element.327, f32[1024,4]{0,1:T(4,128)S(1)} %get-tuple-element.312, pred[]{:T(512)S(6)} %compare.44), kind=kOutput, calls=%fused_computation.7.clone.1 | convolution fusion | flops 550240256 | bytes 19431424 | tf_op jit(solution)/shard_map/while/body/eval_jaxpr/hqk,khd->qhd/dot_general | solution.py:109
  227.2 8.5 %fusion.165 = f32[4,1024]{1,0:T(4,128)S(1)} fusion(f32[4,1024,1024]{2,1,0:T(8,128)} %get-tuple-element.310, f32[4,1024]{1,0:T(4,128)S(1)} %get-tuple-element.336), kind=kLoop, calls=%fused_computation.4.clone.1 | loop fusion | flops 12578816 | bytes 16809984 | tf_op jit(solution)/shard_map/while/body/eval_jaxpr/reduce_sum | solution.py:108
  237.1 8.1 %bitcast_reduce_fusion.2 = (f32[4,1024]{1,0:T(4,128)S(1)}, f32[4,1024,1024]{2,1,0:T(8,128)}) fusion(bf16[1024,4,64]{0,2,1:T(8,128)(2,1)S(1)} %bitcast.131, bf16[1024,4,64]{0,2,1:T(8,128)(2,1)S(1)} %get-tuple-element.340), kind=kOutput, calls=%fused_computation.1.clone.1 | convolution fusion | flops 545255424 | bytes 17842176 | tf_op jit(solution)/shard_map/while/body/eval_jaxpr/qhd,khd->hqk/dot_general | solution.py:102
  245.2 7.4 %fusion.167 = f32[1024,4,64]{0,2,1:T(8,128)S(1)} fusion(bf16[1024,4,64]{0,2,1:T(8,128)(2,1)S(1)} %bitcast.132, f32[4,1024,1024]{2,1,0:T(8,128)} %get-tuple-element.310, f32[4,1024]{1,0:T(4,128)S(1)} %get-tuple-element.336, f32[1024,4,64]{0,2,1:T(8,128)S(1)} %get-tuple-element.327, f32[1024,4]{0,1:T(4,128)S(1)} %get-tuple-element.312, pred[]{:T(512)S(6)} %compare.44), kind=kOutput, calls=%fused_computation.7.clone.1 | convolution fusion | flops 550240256 | bytes 19431424 | tf_op jit(solution)/shard_map/while/body/eval_jaxpr/hqk,khd->qhd/dot_general | solution.py:109
  252.6 8.5 %fusion.165 = f32[4,1024]{1,0:T(4,128)S(1)} fusion(f32[4,1024,1024]{2,1,0:T(8,128)} %get-tuple-element.310, f32[4,1024]{1,0:T(4,128)S(1)} %get-tuple-element.336), kind=kLoop, calls=%fused_computation.4.clone.1 | loop fusion | flops 12578816 | bytes 16809984 | tf_op jit(solution)/shard_map/while/body/eval_jaxpr/reduce_sum | solution.py:108
  262.5 8.1 %bitcast_reduce_fusion.2 = (f32[4,1024]{1,0:T(4,128)S(1)}, f32[4,1024,1024]{2,1,0:T(8,128)}) fusion(bf16[1024,4,64]{0,2,1:T(8,128)(2,1)S(1)} %bitcast.131, bf16[1024,4,64]{0,2,1:T(8,128)(2,1)S(1)} %get-tuple-element.340), kind=kOutput, calls=%fused_computation.1.clone.1 | convolution fusion | flops 545255424 | bytes 17842176 | tf_op jit(solution)/shard_map/while/body/eval_jaxpr/qhd,khd->hqk/dot_general | solution.py:102
  270.6 7.4 %fusion.167 = f32[1024,4,64]{0,2,1:T(8,128)S(1)} fusion(bf16[1024,4,64]{0,2,1:T(8,128)(2,1)S(1)} %bitcast.132, f32[4,1024,1024]{2,1,0:T(8,128)} %get-tuple-element.310, f32[4,1024]{1,0:T(4,128)S(1)} %get-tuple-element.336, f32[1024,4,64]{0,2,1:T(8,128)S(1)} %get-tuple-element.327, f32[1024,4]{0,1:T(4,128)S(1)} %get-tuple-element.312, pred[]{:T(512)S(6)} %compare.44), kind=kOutput, calls=%fused_computation.7.clone.1 | convolution fusion | flops 550240256 | bytes 19431424 | tf_op jit(solution)/shard_map/while/body/eval_jaxpr/hqk,khd->qhd/dot_general | solution.py:109
  278.0 8.5 %fusion.165 = f32[4,1024]{1,0:T(4,128)S(1)} fusion(f32[4,1024,1024]{2,1,0:T(8,128)} %get-tuple-element.310, f32[4,1024]{1,0:T(4,128)S(1)} %get-tuple-element.336), kind=kLoop, calls=%fused_computation.4.clone.1 | loop fusion | flops 12578816 | bytes 16809984 | tf_op jit(solution)/shard_map/while/body/eval_jaxpr/reduce_sum | solution.py:108
  288.5 32.6 %reduce-scatter.2.cloned.1.call-done = bf16[128,128]{1,0:T(8,128)(2,1)} async-done(((bf16[1024,128]{1,0:T(8,128)(2,1)}), bf16[128,128]{1,0:T(8,128)(2,1)}) %reduce-scatter.2.cloned.1.call-update) | async-done | bytes 32784 | tf_op jit(solution)/shard_map/reduce_scatter | solution.py:153
  (144 shorter events, 49.5 us)
Async XLA Ops:
  6.5 82.3 %copy-start = (bf16[128,2048]{1,0:T(8,128)(2,1)S(1)}, bf16[128,2048]{1,0:T(8,128)(2,1)}, u32[]{:S(2)}) copy-start(bf16[128,2048]{1,0:T(8,128)(2,1)} %param.23) | copy-start | bytes 1572868
  6.5 178.4 %all-gather.2.cloned.1.call-start = ((), (), s32[]{:S(2)}) async-start(), calls=%async_computation.1 | async-start | bytes 2621440 | tf_op jit(solution)/shard_map/all_gather | solution.py:88
  6.5 10.9 %collective-permute-start = (bf16[1,4,128,256]{3,2,1,0:T(8,128)(2,1)}, bf16[1,4,128,256]{3,2,1,0:T(8,128)(2,1)S(1)}, u32[]{:S(2)}, u32[]{:S(2)}) collective-permute-start(bf16[1,4,128,256]{3,2,1,0:T(8,128)(2,1)} %param.16), channel_id=1, source_target_pairs={{0,8},{8,16},{16,24},{1,9},{9,17},{17,25},{2,10},{10,18},{18,26},{... | collective-permute-start | bytes 786440 | tf_op jit(solution)/shard_map/ppermute | solution.py:31
  11.6 9.9 %collective-permute-start.1 = (bf16[1,4,128,256]{3,2,1,0:T(8,128)(2,1)}, bf16[1,4,128,256]{3,2,1,0:T(8,128)(2,1)S(1)}, u32[]{:S(2)}, u32[]{:S(2)}) collective-permute-start(bf16[1,4,128,256]{3,2,1,0:T(8,128)(2,1)} %param.16), channel_id=1, source_target_pairs={{8,0},{16,8},{24,16},{9,1},{17,9},{25,17},{10,2},{18,10},{26,18},{... | collective-permute-start | bytes 786440 | tf_op jit(solution)/shard_map/ppermute | solution.py:33
  21.6 4.8 %collective-permute-start.2 = (bf16[3,1,128,256]{3,2,1,0:T(8,128)(2,1)S(1)}, bf16[3,1,128,256]{3,2,1,0:T(8,128)(2,1)S(1)}, u32[]{:S(2)}, u32[]{:S(2)}) collective-permute-start(bf16[3,1,128,256]{3,2,1,0:T(8,128)(2,1)S(1)} %get-tuple-element.248), channel_id=1, source_target_pairs={{0,1},{1,2},{2,3},{3,4},{4,5},{5,6},{6,7},{8,9},{9,10},{10,11},{11... | collective-permute-start | bytes 589832 | tf_op jit(solution)/shard_map/ppermute | solution.py:31
  22.9 5.1 %collective-permute-start.3 = (bf16[3,1,128,256]{3,2,1,0:T(8,128)(2,1)S(1)}, bf16[3,1,128,256]{3,2,1,0:T(8,128)(2,1)S(1)}, u32[]{:S(2)}, u32[]{:S(2)}) collective-permute-start(bf16[3,1,128,256]{3,2,1,0:T(8,128)(2,1)S(1)} %get-tuple-element.247), channel_id=1, source_target_pairs={{1,0},{2,1},{3,2},{4,3},{5,4},{6,5},{7,6},{9,8},{10,9},{11,10},{12... | collective-permute-start | bytes 589832 | tf_op jit(solution)/shard_map/ppermute | solution.py:33
  33.5 22.6 %copy-start.2 = (bf16[3,3,3,256,256]{4,3,2,1,0:T(8,128)(2,1)S(1)}, bf16[3,3,3,256,256]{4,3,2,1,0:T(8,128)(2,1)}, u32[]{:S(2)}) copy-start(bf16[3,3,3,256,256]{4,3,2,1,0:T(8,128)(2,1)} %param.19) | copy-start | bytes 10616836
  36.8 7.3 %collective-permute-start.4 = (bf16[1,4,128,256]{3,2,1,0:T(8,128)(2,1)S(1)}, bf16[1,4,128,256]{3,2,1,0:T(8,128)(2,1)S(1)}, u32[]{:S(2)}, u32[]{:S(2)}) collective-permute-start(bf16[1,4,128,256]{3,2,1,0:T(8,128)(2,1)S(1)} %fusion.66), channel_id=1, source_target_pairs={{0,8},{8,16},{16,24},{1,9},{9,17},{17,25},{2,10},{10,18},{18,26},{... | collective-permute-start | bytes 786440 | tf_op jit(solution)/shard_map/ppermute | solution.py:31
  40.3 8.3 %collective-permute-start.5 = (bf16[1,4,128,256]{3,2,1,0:T(8,128)(2,1)S(1)}, bf16[1,4,128,256]{3,2,1,0:T(8,128)(2,1)S(1)}, u32[]{:S(2)}, u32[]{:S(2)}) collective-permute-start(bf16[1,4,128,256]{3,2,1,0:T(8,128)(2,1)S(1)} %fusion.66), channel_id=1, source_target_pairs={{8,0},{16,8},{24,16},{9,1},{17,9},{25,17},{10,2},{18,10},{26,18},{... | collective-permute-start | bytes 786440 | tf_op jit(solution)/shard_map/ppermute | solution.py:33
  49.3 9.0 %collective-permute-start.6 = (bf16[3,1,128,256]{3,2,1,0:T(8,128)(2,1)}, bf16[3,1,128,256]{3,2,1,0:T(8,128)(2,1)}, u32[]{:S(2)}, u32[]{:S(2)}) collective-permute-start(bf16[3,1,128,256]{3,2,1,0:T(8,128)(2,1)} %get-tuple-element.246), channel_id=1, source_target_pairs={{0,1},{1,2},{2,3},{3,4},{4,5},{5,6},{6,7},{8,9},{9,10},{10,11},{11... | collective-permute-start | bytes 589832 | tf_op jit(solution)/shard_map/ppermute | solution.py:31
  54.6 5.0 %collective-permute-start.7 = (bf16[3,1,128,256]{3,2,1,0:T(8,128)(2,1)}, bf16[3,1,128,256]{3,2,1,0:T(8,128)(2,1)S(1)}, u32[]{:S(2)}, u32[]{:S(2)}) collective-permute-start(bf16[3,1,128,256]{3,2,1,0:T(8,128)(2,1)} %get-tuple-element.245), channel_id=1, source_target_pairs={{1,0},{2,1},{3,2},{4,3},{5,4},{6,5},{7,6},{9,8},{10,9},{11,10},{12... | collective-permute-start | bytes 589832 | tf_op jit(solution)/shard_map/ppermute | solution.py:33
  59.7 2.4 copy-start.12
  62.1 1.1 copy-start.10
  63.3 1.0 copy-start.9
  64.9 1.1 copy-start.7
  66.0 1.1 copy-start.25
  66.4 1.0 copy-start.6
  67.5 1.0 copy-start.5
  68.8 1.0 copy-start.18
  70.9 2.7 copy-start.15
  70.9 2.7 copy-start.19
  70.9 17.9 %copy-start.16 = (f32[2048]{0:T(1024)S(1)}, f32[2048]{0:T(1024)}, u32[]{:S(2)}) copy-start(f32[2048]{0:T(1024)} %param.24) | copy-start | bytes 24580
  90.2 1.3 copy-start.20
  90.2 1.5 copy-start.21
  90.2 1.8 copy-start.22
  90.2 1.8 copy-start.23
  96.4 16.0 %collective-permute-start.8 = (bf16[1024,256]{0,1:T(8,128)(2,1)S(1)}, bf16[1024,256]{0,1:T(8,128)(2,1)S(1)}, u32[]{:S(2)}, u32[]{:S(2)}) collective-permute-start(bf16[1024,256]{0,1:T(8,128)(2,1)S(1)} %slice.446), channel_id=1, source_target_pairs={{0,8},{8,16},{16,24},{24,0},{1,9},{9,17},{17,25},{25,1},{2,10},{10... | collective-permute-start | bytes 1572872 | tf_op jit(solution)/shard_map/ppermute | solution.py:16
  112.4 16.6 %collective-permute-start.9 = (bf16[1024,256]{0,1:T(8,128)(2,1)S(1)}, bf16[1024,256]{0,1:T(8,128)(2,1)S(1)}, u32[]{:S(2)}, u32[]{:S(2)}) collective-permute-start(bf16[1024,256]{0,1:T(8,128)(2,1)S(1)} %collective-permute-done.8), channel_id=1, source_target_pairs={{0,8},{8,16},{16,24},{24,0},{1,9},{9,17},{17,25},{25,1},{2,10},{10... | collective-permute-start | bytes 1572872 | tf_op jit(solution)/shard_map/ppermute | solution.py:16
  112.4 24.6 %collective-permute-start.10 = (bf16[1024,256]{0,1:T(8,128)(2,1)S(1)}, bf16[1024,256]{0,1:T(8,128)(2,1)S(1)}, u32[]{:S(2)}, u32[]{:S(2)}) collective-permute-start(bf16[1024,256]{0,1:T(8,128)(2,1)S(1)} %slice.446), channel_id=1, source_target_pairs={{0,24},{8,0},{16,8},{24,16},{1,25},{9,1},{17,9},{25,17},{2,26},{10... | collective-permute-start | bytes 1572872 | tf_op jit(solution)/shard_map/ppermute | solution.py:18
  138.1 2.0 copy-start.3
  140.0 181.1 %reduce-scatter.2.cloned.1.call-start = ((), (), s32[]{:S(2)}) async-start(), calls=%async_computation.2 | async-start | bytes 294912 | tf_op jit(solution)/shard_map/reduce_scatter | solution.py:153
  286.6 36.0 %copy-start.1 = (bf16[128,2048]{1,0:T(8,128)(2,1)S(1)}, bf16[128,2048]{1,0:T(8,128)(2,1)}, u32[]{:S(2)}) copy-start(bf16[128,2048]{1,0:T(8,128)(2,1)} %param.23) | copy-start | bytes 1572868
  (7 other events, 6.5 us)
Sparse Core Ops, SparseCore 0:
  140.2 44.7 all-gather.1
  288.7 32.4 reduce-scatter.1
